TPU v7x, 32 devices: a whole 2x2x4 slice. The times are simulated.
32 devices in a mesh: dp: 8 (over z, x), tensor: 4 (over y, core).
Axes of the slice: x: 2, y: 2, z: 4, core: 2. Of those that a mesh axis runs over, the one named last changes fastest.
Arguments:
- source_rows: bfloat16 [2, 2048, 3072], P(None, ('dp', 'tensor')), may hold values from -6 to 6
- gate_weight: bfloat16 [2, 3072, 9216], P(None, 'dp', 'tensor'), may hold values from -0.15625 to 0.15625
- up_weight: bfloat16 [2, 3072, 9216], P(None, 'dp', 'tensor'), may hold values from -0.15625 to 0.15625
- keep_mask: int32 [2, 2, 48, 144], replicated, may hold values from 0 to 1, as said below
Outputs:
- hidden: bfloat16 [2, 2048, 9216], P(None, 'dp', 'tensor')
Inputs may be any that keep to these rules, and one draw needn't show every extreme that they name: `keep_mask`: within each device's share of a projection (6 x 36 blocks: block rows of one dp index, block columns of one tensor index) at least one and at most 108 blocks are kept, and for each direction and projection some share keeps exactly 108.
All inputs are finite; a program needn't handle non-finite values.
Results may differ from a plain program's by a relative error of at most 0.001.
Values may be sent and summed in bfloat16 or wider, within the bound.
No kernel may reach another device: no remote copies, remote signals or barrier semaphores. Data moves between devices by JAX's collectives and lax.ppermute only.
A program may use at most 192 MiB of HBM per device.

v0:
```python
import jax
import jax.numpy as jnp
from jax import lax
from jax.sharding import PartitionSpec as P

BLOCK = 64


def expand_blocks(block_mask, block_width):
    return jnp.repeat(jnp.repeat(block_mask, block_width, axis=-2), block_width, axis=-1)


def shards(source_rows, gate_weight, up_weight, keep_mask):
    token_slab = lax.all_gather(source_rows, "tensor", axis=1, tiled=True)
    row_blocks = gate_weight.shape[1] // BLOCK
    col_blocks = gate_weight.shape[2] // BLOCK
    dp_index = lax.axis_index("dp")
    tensor_index = lax.axis_index("tensor")
    mask_cols = lax.dynamic_slice_in_dim(keep_mask, tensor_index * col_blocks, col_blocks, 3)
    own_mask = lax.dynamic_slice_in_dim(mask_cols, dp_index * row_blocks, row_blocks, 2)
    stacked = jnp.stack([gate_weight, up_weight], axis=1)
    kept_rows = stacked * expand_blocks(own_mask, BLOCK).astype(jnp.bfloat16)
    weights = lax.all_gather(kept_rows, "dp", axis=2, tiled=True)
    gate_sum = jnp.einsum(
        "mgd,mdf->mgf", token_slab, weights[:, 0], preferred_element_type=jnp.float32
    )
    up_sum = jnp.einsum(
        "mgd,mdf->mgf", token_slab, weights[:, 1], preferred_element_type=jnp.float32
    )
    return (jax.nn.silu(gate_sum) * up_sum).astype(jnp.bfloat16)


def solution(mesh):
    placed = (
        P(None, ("dp", "tensor"), None),
        P(None, "dp", "tensor"),
        P(None, "dp", "tensor"),
        P(),
    )
    return jax.shard_map(
        shards, mesh=mesh, in_specs=placed, out_specs=P(None, "dp", "tensor"), check_vma=False
    )
```

profile of v0, /device:TPU:0, one launch (start us, length us, event | category | flops | bytes accessed | tf_op | source)
XLA Modules:
  0.0 1152.1 jit_solution(3198824043148178128)
XLA Ops:
  6.5 0.0 all-gather.5.cloned.1.call-start
  6.5 0.7 all-gather.5.cloned.1.call-update
  7.3 0.0 all-gather.3.cloned.1.call-start
  7.3 0.9 dynamic-slice_convert_fusion
  8.2 0.1 copy.11
  8.4 0.2 broadcast_in_dim.6
  8.6 0.2 convert_element_type.15
  8.8 0.7 copy.12
  9.5 4.6 copy.9
  14.1 5.8 copy.10
  20.0 5.9 maximum_multiply_fusion
  25.9 0.0 all-gather.3.cloned.1.call-update
  26.0 14.2 %all-gather.5.cloned.1.call-done = bf16[2,256,3072]{2,1,0:T(8,128)(2,1)} async-done(((bf16[2,64,3072]{2,1,0:T(8,128)(2,1)}), bf16[2,256,3072]{2,1,0:T(8,128)(2,1)}) %all-gather.5.cloned.1.call-update) | async-done | bytes 3145744 | tf_op jit(solution)/shard_map/all_gather | solution.py:14
  40.2 1071.8 %all-gather.3.cloned.1.call-done = bf16[2,2,3072,2304]{2,3,0,1:T(8,128)(2,1)} async-done(((bf16[2,2,384,2304]{2,3,0,1:T(8,128)(2,1)}), bf16[2,2,3072,2304]{2,3,0,1:T(8,128)(2,1)}) %all-gather.3.cloned.1.call-update) | async-done | bytes 56623120 | tf_op jit(solution)/shard_map/all_gather | solution.py:23
  1112.0 15.3 %fusion.2 = f32[2,256,2304]{1,2,0:T(8,128)} fusion(bf16[2,256,3072]{2,1,0:T(8,128)(2,1)} %all-gather.5.cloned.1.call-done, bf16[2,2,3072,2304]{2,3,0,1:T(8,128)(2,1)} %all-gather.3.cloned.1.call-done), kind=kOutput, calls=%fused_computation.5 | convolution fusion | flops 7247757312 | bytes 36175872 | tf_op jit(solution)/shard_map/mgd,mdf->mgf/dot_general | solution.py:24
  1127.2 15.6 %fusion.5 = bf16[2,256,2304]{1,2,0:T(8,128)(2,1)S(1)} fusion(bf16[2,256,3072]{2,1,0:T(8,128)(2,1)} %all-gather.5.cloned.1.call-done, bf16[2,2,3072,2304]{2,3,0,1:T(8,128)(2,1)} %all-gather.3.cloned.1.call-done, f32[2,256,2304]{1,2,0:T(8,128)} %fusion.2), kind=kOutput, calls=%fused_computation.8 | convolution fusion | flops 7254835200 | bytes 38535168 | tf_op jit(solution)/shard_map/mgd,mdf->mgf/dot_general | solution.py:27
  1142.9 2.4 copy.13
Async XLA Ops:
  6.5 33.6 %all-gather.5.cloned.1.call-start = ((), (), s32[]{:S(2)}) async-start(), calls=%async_computation.1 | async-start | bytes 3932160 | tf_op jit(solution)/shard_map/all_gather | solution.py:14
  7.3 1104.7 %all-gather.3.cloned.1.call-start = ((), (), s32[]{:S(2)}) async-start(), calls=%async_computation | async-start | bytes 63700992 | tf_op jit(solution)/shard_map/all_gather | solution.py:23
Sparse Core Ops, SparseCore 0:
  8.9 31.2 all-gather.4
  41.7 1070.2 all-gather.2
where the time goes:
time: 1150 us
  waiting for transfers between devices  1090 us (95%)
  matrix products  30.9 us (3%)
  local copies, waits for them, and re-layouts  14.2 us (1%)
  between operations  13.4 us (1%)
    all_gather x1, waiting for transfers between devices, shards(): weights = lax.all_gather(kept_rows, 'dp', axis=2, tiled=True)  1070 us
  transfers between devices with their start and end apart: 2, of which 2 were waited for; matrix products, arithmetic and copies ran while one was open for 2% of the time, Pallas kernels for 0%

commit v1 on v0

--- a/solution.py
+++ b/solution.py
@@ -4,6 +4,17 @@
 from jax.sharding import PartitionSpec as P
 
 BLOCK = 64
+
+
+def gather_around(x, axis, dim):
+    ways = lax.axis_size(axis)
+    pieces = [x]
+    for far in range(1, ways):
+        pieces.append(
+            lax.ppermute(pieces[far - 1], axis, [(d, (d - 1) % ways) for d in range(ways)])
+        )
+    line = jnp.concatenate(pieces, axis=dim)
+    return jnp.roll(line, lax.axis_index(axis) * x.shape[dim], axis=dim)
 
 
 def expand_blocks(block_mask, block_width):
@@ -20,7 +31,7 @@
     own_mask = lax.dynamic_slice_in_dim(mask_cols, dp_index * row_blocks, row_blocks, 2)
     stacked = jnp.stack([gate_weight, up_weight], axis=1)
     kept_rows = stacked * expand_blocks(own_mask, BLOCK).astype(jnp.bfloat16)
-    weights = lax.all_gather(kept_rows, "dp", axis=2, tiled=True)
+    weights = gather_around(kept_rows, "dp", 2)
     gate_sum = jnp.einsum(
         "mgd,mdf->mgf", token_slab, weights[:, 0], preferred_element_type=jnp.float32
     )

time: 1150 us -> 1220 us (1.061)
  local copies, waits for them, and re-layouts: 14.2 us -> 113 us
  waiting for transfers between devices: 1090 us -> 1010 us
  starting transfers between devices: 0.04 us -> 37 us
    all_gather x1 -> x0, waiting for transfers between devices: 1070 us -> none  [shards(): weights = lax.all_gather(kept_rows, 'dp', axis=2, tiled=True)]
    ppermute x0 -> x7, waiting for transfers between devices: none -> 1010 us  [gather_around(): lax.ppermute(pieces[far - 1], axis, [(d, (d - 1) % ways) for d in range(w...]
    unnamed x2 -> x50, local copies, waits for them, and re-layouts: 10.5 us -> 103 us
    ppermute x0 -> x7, starting transfers between devices: none -> 37 us  [gather_around(): lax.ppermute(pieces[far - 1], axis, [(d, (d - 1) % ways) for d in range(w...]
    all_gather x1, waiting for transfers between devices: 14.2 us -> 0.01 us  [shards(): token_slab = lax.all_gather(source_rows, 'tensor', axis=1, tiled=True)]
  transfers between devices with their start and end apart: 2 -> 8, of which waited for: 2 -> 7; matrix products, arithmetic and copies ran while one was open for 2% -> 7% of each run, Pallas kernels for 0% -> 0%
where the time goes in v1:
time: 1220 us
  waiting for transfers between devices  1010 us (83%)
  local copies, waits for them, and re-layouts  113 us (9%)
  matrix products  37.5 us (3%)
  starting transfers between devices  37 us (3%)
  between operations  13.5 us (1%)
    ppermute x7, waiting for transfers between devices, gather_around(): lax.ppermute(pieces[far - 1], axis, [(d, (d - 1) % ways) for d in range(w...  1010 us
    unnamed x50, local copies, waits for them, and re-layouts  103 us
    ppermute x7, starting transfers between devices, gather_around(): lax.ppermute(pieces[far - 1], axis, [(d, (d - 1) % ways) for d in range(w...  37 us
  transfers between devices with their start and end apart: 8, of which 7 were waited for; matrix products, arithmetic and copies ran while one was open for 7% of the time, Pallas kernels for 0%

profile of v1, /device:TPU:0, one launch (start us, length us, event | category | flops | bytes accessed | tf_op | source)
XLA Modules:
  0.0 1217.6 jit_solution(6836514860711163510)
XLA Ops:
  13.3 5.8 copy.10
  19.1 7.2 constant_dynamic-update-slice_fusion.15
  26.3 5.9 collective-permute-start
  32.2 151.9 %collective-permute-done = bf16[2,2,384,2304]{2,3,0,1:T(8,128)(2,1)S(1)} collective-permute-done((bf16[2,2,384,2304]{2,3,0,1:T(8,128)(2,1)}, bf16[2,2,384,2304]{2,3,0,1:T(8,128)(2,1)S(1)}, u32[]{:S(2)}, u32[]{:S(2)}) %collective-permute-start) | collective-permute-done | bytes 7077920 | tf_op jit(solution)/shard_map/ppermute | solution.py:14
  192.2 150.8 %collective-permute-done.1 = bf16[2,2,384,2304]{2,3,0,1:T(8,128)(2,1)S(1)} collective-permute-done((bf16[2,2,384,2304]{2,3,0,1:T(8,128)(2,1)S(1)}, bf16[2,2,384,2304]{2,3,0,1:T(8,128)(2,1)S(1)}, u32[]{:S(2)}, u32[]{:S(2)}) %collective-permute-start.1) | collective-permute-done | bytes 7077920 | tf_op jit(solution)/shard_map/ppermute | solution.py:14
  345.8 5.2 collective-permute-start.2
  351.0 149.9 %collective-permute-done.2 = bf16[2,2,384,2304]{2,3,0,1:T(8,128)(2,1)S(1)} collective-permute-done((bf16[2,2,384,2304]{2,3,0,1:T(8,128)(2,1)S(1)}, bf16[2,2,384,2304]{2,3,0,1:T(8,128)(2,1)S(1)}, u32[]{:S(2)}, u32[]{:S(2)}) %collective-permute-start.2) | collective-permute-done | bytes 7077920 | tf_op jit(solution)/shard_map/ppermute | solution.py:14
  503.8 5.2 collective-permute-start.3
  509.0 149.1 %collective-permute-done.3 = bf16[2,2,384,2304]{2,3,0,1:T(8,128)(2,1)S(1)} collective-permute-done((bf16[2,2,384,2304]{2,3,0,1:T(8,128)(2,1)S(1)}, bf16[2,2,384,2304]{2,3,0,1:T(8,128)(2,1)S(1)}, u32[]{:S(2)}, u32[]{:S(2)}) %collective-permute-start.3) | collective-permute-done | bytes 7077920 | tf_op jit(solution)/shard_map/ppermute | solution.py:14
  666.1 148.2 %collective-permute-done.4 = bf16[2,2,384,2304]{2,3,0,1:T(8,128)(2,1)S(1)} collective-permute-done((bf16[2,2,384,2304]{2,3,0,1:T(8,128)(2,1)S(1)}, bf16[2,2,384,2304]{2,3,0,1:T(8,128)(2,1)S(1)}, u32[]{:S(2)}, u32[]{:S(2)}) %collective-permute-start.4) | collective-permute-done | bytes 7077920 | tf_op jit(solution)/shard_map/ppermute | solution.py:14
  822.3 147.3 %collective-permute-done.5 = bf16[2,2,384,2304]{2,3,0,1:T(8,128)(2,1)} collective-permute-done((bf16[2,2,384,2304]{2,3,0,1:T(8,128)(2,1)S(1)}, bf16[2,2,384,2304]{2,3,0,1:T(8,128)(2,1)}, u32[]{:S(2)}, u32[]{:S(2)}) %collective-permute-start.5) | collective-permute-done | bytes 7077920 | tf_op jit(solution)/shard_map/ppermute | solution.py:14
  969.6 5.3 collective-permute-start.6
  975.0 7.1 constant_dynamic-update-slice_fusion.14
  985.9 7.0 constant_dynamic-update-slice_fusion.12
  992.9 7.0 constant_dynamic-update-slice_fusion.11
  1003.8 7.0 constant_dynamic-update-slice_fusion.9
  1010.8 110.9 %collective-permute-done.6 = bf16[2,2,384,2304]{2,3,0,1:T(8,128)(2,1)} collective-permute-done((bf16[2,2,384,2304]{2,3,0,1:T(8,128)(2,1)}, bf16[2,2,384,2304]{2,3,0,1:T(8,128)(2,1)}, u32[]{:S(2)}, u32[]{:S(2)}) %collective-permute-start.6) | collective-permute-done | bytes 7077920 | tf_op jit(solution)/shard_map/ppermute | solution.py:14
  1121.7 6.7 constant_dynamic-update-slice_fusion.8
  1136.0 7.0 constant_dynamic-update-slice_fusion.5
  1150.3 6.8 constant_dynamic-update-slice_fusion.2
  1157.1 6.9 constant_dynamic-update-slice_fusion.1
  1164.0 6.8 constant_dynamic-update-slice_fusion
  1170.8 18.8 %fusion.2 = f32[2,256,2304]{1,2,0:T(8,128)} fusion(bf16[2,256,3072]{2,1,0:T(8,128)(2,1)} %all-gather.2.cloned.1.call-done, bf16[2,2,6144,2304]{2,3,0,1:T(8,128)(2,1)} %constant_dynamic-update-slice_fusion, s32[]{:T(128)S(6)} %select_n.28), kind=kOutput, calls=%fused_computation.5 | convolution fusion | flops 7247757312 | bytes 36175876 | tf_op jit(solution)/shard_map/mgd,mdf->mgf/dot_general | solution.py:35
  1189.5 18.8 %multiply_convert_fusion = bf16[2,256,2304]{1,2,0:T(8,128)(2,1)S(1)} fusion(f32[2,256,2304]{1,2,0:T(8,128)} %fusion.2, bf16[2,256,3072]{2,1,0:T(8,128)(2,1)} %all-gather.2.cloned.1.call-done, bf16[2,2,6144,2304]{2,3,0,1:T(8,128)(2,1)} %constant_dynamic-update-slice_fusion, s32[]{:T(128)S(6)} %add.29, s32[]{:T(128)S(6)} %select_n.28), kind=kOutput, calls=%fused_computation.7 | convolution fusion | flops 7254835200 | bytes 38535176 | tf_op jit(solution)/shard_map/mgd,mdf->mgf/dot_general | solution.py:38
  (59 shorter events, 61.6 us)
Async XLA Ops:
  6.5 1164.2 %all-gather.2.cloned.1.call-start = ((), (), s32[]{:S(2)}) async-start(), calls=%async_computation | async-start | bytes 3932160 | tf_op jit(solution)/shard_map/all_gather | solution.py:25
  26.3 157.9 %collective-permute-start = (bf16[2,2,384,2304]{2,3,0,1:T(8,128)(2,1)}, bf16[2,2,384,2304]{2,3,0,1:T(8,128)(2,1)S(1)}, u32[]{:S(2)}, u32[]{:S(2)}) collective-permute-start(bf16[2,2,384,2304]{2,3,0,1:T(8,128)(2,1)} %get-tuple-element.6), channel_id=1, source_target_pairs={{0,28},{4,0},{8,4},{12,8},{16,12},{20,16},{24,20},{28,24},{1,29},{... | collective-permute-start | bytes 21233672 | tf_op jit(solution)/shard_map/ppermute | solution.py:14
  184.2 2.9 copy-start
  187.1 155.8 %collective-permute-start.1 = (bf16[2,2,384,2304]{2,3,0,1:T(8,128)(2,1)S(1)}, bf16[2,2,384,2304]{2,3,0,1:T(8,128)(2,1)S(1)}, u32[]{:S(2)}, u32[]{:S(2)}) collective-permute-start(bf16[2,2,384,2304]{2,3,0,1:T(8,128)(2,1)S(1)} %collective-permute-done), channel_id=1, source_target_pairs={{0,28},{4,0},{8,4},{12,8},{16,12},{20,16},{24,20},{28,24},{1,29},{... | collective-permute-start | bytes 21233672 | tf_op jit(solution)/shard_map/ppermute | solution.py:14
  342.9 2.9 copy-start.1
  345.8 155.1 %collective-permute-start.2 = (bf16[2,2,384,2304]{2,3,0,1:T(8,128)(2,1)S(1)}, bf16[2,2,384,2304]{2,3,0,1:T(8,128)(2,1)S(1)}, u32[]{:S(2)}, u32[]{:S(2)}) collective-permute-start(bf16[2,2,384,2304]{2,3,0,1:T(8,128)(2,1)S(1)} %collective-permute-done.1), channel_id=1, source_target_pairs={{0,28},{4,0},{8,4},{12,8},{16,12},{20,16},{24,20},{28,24},{1,29},{... | collective-permute-start | bytes 21233672 | tf_op jit(solution)/shard_map/ppermute | solution.py:14
  351.0 631.1 %slice-start.4 = ((s8[7077888]{0:T(1024)(128)(4,1)}), s8[2883584]{0:T(1024)(128)(4,1)S(1)}, s32[]{:S(2)}) async-start(s8[7077888]{0:T(1024)(128)(4,1)} %bitcast.30), calls=%async_computation.5 | async-start | bytes 5767168
  500.9 3.0 copy-start.2
  503.8 154.2 %collective-permute-start.3 = (bf16[2,2,384,2304]{2,3,0,1:T(8,128)(2,1)S(1)}, bf16[2,2,384,2304]{2,3,0,1:T(8,128)(2,1)S(1)}, u32[]{:S(2)}, u32[]{:S(2)}) collective-permute-start(bf16[2,2,384,2304]{2,3,0,1:T(8,128)(2,1)S(1)} %collective-permute-done.2), channel_id=1, source_target_pairs={{0,28},{4,0},{8,4},{12,8},{16,12},{20,16},{24,20},{28,24},{1,29},{... | collective-permute-start | bytes 21233672 | tf_op jit(solution)/shard_map/ppermute | solution.py:14
  660.9 153.4 %collective-permute-start.4 = (bf16[2,2,384,2304]{2,3,0,1:T(8,128)(2,1)S(1)}, bf16[2,2,384,2304]{2,3,0,1:T(8,128)(2,1)S(1)}, u32[]{:S(2)}, u32[]{:S(2)}) collective-permute-start(bf16[2,2,384,2304]{2,3,0,1:T(8,128)(2,1)S(1)} %collective-permute-done.3), channel_id=1, source_target_pairs={{0,28},{4,0},{8,4},{12,8},{16,12},{20,16},{24,20},{28,24},{1,29},{... | collective-permute-start | bytes 21233672 | tf_op jit(solution)/shard_map/ppermute | solution.py:14
  814.3 2.8 copy-start.4
  817.1 152.5 %collective-permute-start.5 = (bf16[2,2,384,2304]{2,3,0,1:T(8,128)(2,1)S(1)}, bf16[2,2,384,2304]{2,3,0,1:T(8,128)(2,1)}, u32[]{:S(2)}, u32[]{:S(2)}) collective-permute-start(bf16[2,2,384,2304]{2,3,0,1:T(8,128)(2,1)S(1)} %collective-permute-done.4), channel_id=1, source_target_pairs={{0,28},{4,0},{8,4},{12,8},{16,12},{20,16},{24,20},{28,24},{1,29},{... | collective-permute-start | bytes 21233672 | tf_op jit(solution)/shard_map/ppermute | solution.py:14
  969.6 152.1 %collective-permute-start.6 = (bf16[2,2,384,2304]{2,3,0,1:T(8,128)(2,1)}, bf16[2,2,384,2304]{2,3,0,1:T(8,128)(2,1)}, u32[]{:S(2)}, u32[]{:S(2)}) collective-permute-start(bf16[2,2,384,2304]{2,3,0,1:T(8,128)(2,1)} %collective-permute-done.5), channel_id=1, source_target_pairs={{0,28},{4,0},{8,4},{12,8},{16,12},{20,16},{24,20},{28,24},{1,29},{... | collective-permute-start | bytes 21233672 | tf_op jit(solution)/shard_map/ppermute | solution.py:14
  975.0 7.1 slice-start.5
  985.9 14.0 %slice-start.10 = ((s8[7077888]{0:T(1024)(128)(4,1)}), s8[4194304]{0:T(1024)(128)(4,1)S(1)}, s32[]{:S(2)}) async-start(s8[7077888]{0:T(1024)(128)(4,1)} %bitcast.36), calls=%async_computation.11 | async-start | bytes 8388608
  992.9 7.0 slice-start.11
  1003.8 124.6 %slice-start = ((s8[7077888]{0:T(1024)(128)(4,1)}), s8[4194304]{0:T(1024)(128)(4,1)S(1)}, s32[]{:S(2)}) async-start(s8[7077888]{0:T(1024)(128)(4,1)} %bitcast.26), calls=%async_computation.1 | async-start | bytes 8388608
  1010.8 117.7 %slice-start.1 = ((s8[7077888]{0:T(1024)(128)(4,1)}), s8[2883584]{0:T(1024)(128)(4,1)S(1)}, s32[]{:S(2)}) async-start(s8[7077888]{0:T(1024)(128)(4,1)} %bitcast.26), calls=%async_computation.2 | async-start | bytes 5767168
  1010.8 121.4 %slice-start.2 = ((s8[7077888]{0:T(1024)(128)(4,1)}), s8[4194304]{0:T(1024)(128)(4,1)S(1)}, s32[]{:S(2)}) async-start(s8[7077888]{0:T(1024)(128)(4,1)} %bitcast.28), calls=%async_computation.3 | async-start | bytes 8388608
  1128.5 3.8 slice-start.3
  1132.2 10.7 slice-start.6
  1136.0 7.0 slice-start.7
  1136.0 10.7 slice-start.8
  1143.0 3.7 slice-start.9
  (1 other events, 2.8 us)
Sparse Core Ops, SparseCore 0:
  975.1 25.7 all-gather.1
